TPU v7x, 128 devices: a whole 4x4x4 slice. The times are simulated.
128 devices in a mesh: row: 16 (over x_lo, z, core), col: 8 (over x_hi, y).
Axes of the slice: x: 4 (x_hi: 2, x_lo: 2; x = x_hi * 2 + x_lo), y: 4, z: 4, core: 2. Of those that a mesh axis runs over, the one named last changes fastest.
Arguments:
- eigvecs: float32 [512, 262144], P(('row', 'col')), may hold values from -6 to 6
- panels: bfloat16 [8, 262144, 128], P('col', 'row'), may hold values from -0.01171875 to 0.01171875
- tfactors: bfloat16 [8, 128, 128], P('col'), as said below
- owners: int32 [4], replicated, may hold values from 0 to 7, as said below
- offsets: int32 [4], replicated, may hold values from 0 to 65408, as said below
Outputs:
- back: float32 [512, 262144], P('col', 'row')
Inputs may be any that keep to these rules, and one draw needn't show every extreme that they name: `owners`: distinct grid columns. `offsets`: multiples of 128. `tfactors`: each matrix is upper triangular with its diagonal between 1 and 8.
All inputs are finite; a program needn't handle non-finite values.
Results may differ from a plain program's by a relative error of at most 0.0003.
Values may be sent and summed in bfloat16 or wider, within the bound.
No kernel may reach another device: no remote copies, remote signals or barrier semaphores. Data moves between devices by JAX's collectives and lax.ppermute only.
A program may use at most 128 MiB of HBM per device.

v0:
```python
import jax
import jax.numpy as jnp
from jax import lax
from jax.sharding import PartitionSpec as P

PANELS = 4


def from_root(value, axis, root):
    mine = lax.axis_index(axis) == root
    return lax.psum(jnp.where(mine, value, jnp.zeros_like(value)), axis)


def reflector_block(stored, offset, first_row):
    row_ids = first_row + lax.broadcasted_iota(jnp.int32, stored.shape, 0)
    col_ids = lax.broadcasted_iota(jnp.int32, stored.shape, 1)
    below = row_ids - col_ids - offset
    unit = jnp.where(below == 0, jnp.float32(1.0), jnp.float32(0.0))
    return jnp.where(below > 0, stored.astype(jnp.float32), unit)


def local(eigvecs, panels, tfactors, owners, offsets):
    highest = lax.Precision.HIGHEST
    spread = lax.all_to_all(eigvecs, ("row", "col"), split_axis=1, concat_axis=0, tiled=True)
    field = lax.all_to_all(spread, "col", split_axis=0, concat_axis=1, tiled=True)
    local_rows = field.shape[1]
    first_row = lax.axis_index("row") * local_rows
    for panel in reversed(range(PANELS)):
        stored, triangle = (
            from_root(panels[0], "col", owners[panel]),
            from_root(tfactors[0], "col", owners[panel]),
        )
        reflector = reflector_block(stored, offsets[panel], first_row)
        partial_sum = jnp.dot(
            field, reflector, precision=highest, preferred_element_type=jnp.float32
        )
        projection = lax.psum(partial_sum, "row")
        coeffs = jnp.dot(
            projection,
            triangle.astype(jnp.float32).T,
            precision=highest,
            preferred_element_type=jnp.float32,
        )
        field = field - jnp.dot(
            coeffs, reflector.T, precision=highest, preferred_element_type=jnp.float32
        )
    return field


def solution(mesh):
    in_specs = (P(("row", "col"), None), P("col", "row", None), P("col", None, None), P(), P())
    out_specs = P("col", "row")
    return jax.shard_map(local, mesh=mesh, in_specs=in_specs, out_specs=out_specs, check_vma=False)
```

profile of v0, /device:TPU:0, one launch (start us, length us, event | category | flops | bytes accessed | tf_op | source)
XLA Modules:
  0.0 801.4 jit_solution(956062788617892617)
XLA Ops:
  6.5 1.5 fusion.82
  10.5 7.4 select_bitcast_fusion
  18.0 221.5 %all_to_all.35 = f32[4,128,2048]{2,0,1:T(4,128)} all-to-all(f32[4,128,2048]{2,0,1:T(4,128)} %bitcast.48), channel_id=1, replica_groups=mesh['row'=16,'col'=8] {'row','col'}, dimensions={1} | all-to-all | bytes 8388608 | tf_op jit(solution)/shard_map/all_to_all | solution.py:24
  239.5 5.3 all_to_all.29
  244.8 4.7 all-to-all-start.1
  249.5 0.0 all-reduce.5.cloned.1.call-start
  249.6 0.7 select_bitcast_fusion.4
  250.2 0.0 all-reduce.5.cloned.1.call-update
  250.3 0.7 fusion.81
  251.0 99.6 %all-to-all-done.1 = f32[8,64,2048]{2,1,0:T(8,128)} async-done(((f32[8,64,2048]{2,1,0:T(8,128)}), f32[8,64,2048]{2,1,0:T(8,128)}, u32[]{:S(2)}, u32[]{:S(2)}) %all-to-all-start.1) | async-done | bytes 4194336 | tf_op jit(solution)/shard_map/all_to_all | solution.py:25
  350.6 4.7 copy.8
  355.3 106.0 %all-reduce.7.cloned.1.call-done = (bf16[16384,128]{1,0:T(8,128)(2,1)}, bf16[16384,128]{1,0:T(8,128)(2,1)}, bf16[16384,128]{1,0:T(8,128)(2,1)}, bf16[16384,128]{1,0:T(8,128)(2,1)}) async-done(((bf16[16384,128]{1,0:T(8,128)(2,1)}, bf16[16384,128]{1,0:T(8,128)(2,1)}, bf16[16384,128]{1,0:T(8,128)(2,1)}, bf16[16384,128]{1,0:T(8,128)(2,1)}), (bf16[16384,128]{1,0:T(8,128)(2,1)}, bf16[16384,128]{1,0:T(8,128)(2,1)}, ...) | async-done | bytes 16777232 | tf_op jit(solution)/shard_map/psum | solution.py:11
  461.3 16.5 %fusion.56 = f32[64,128]{0,1:T(8,128)S(1)} fusion(f32[64,16384]{1,0:T(8,128)} %bitcast.49, bf16[16384,128]{1,0:T(8,128)(2,1)} %get-tuple-element.9, s32[]{:T(128)} %bitcast.3, s32[16384]{0:T(1024)S(1)} %iota_add_fusion), kind=kOutput, calls=%fused_computation.69 | convolution fusion | flops 1625292800 | bytes 8486916 | tf_op jit(solution)/shard_map/dot_general | solution.py:34
  477.8 55.1 %psum.85 = f32[64,128]{0,1:T(8,128)S(1)} all-reduce(f32[64,128]{0,1:T(8,128)S(1)} %fusion.56), channel_id=1, replica_groups=mesh['row'=16,'col'=8] {'row'}, use_global_device_ids=true, to_apply=%region_1.2 | all-reduce | flops 8192 | bytes 65536 | tf_op jit(solution)/shard_map/psum | solution.py:37
  532.8 18.0 %all-reduce.5.cloned.1.call-done = (bf16[128,128]{1,0:T(8,128)(2,1)}, bf16[128,128]{1,0:T(8,128)(2,1)}, bf16[128,128]{1,0:T(8,128)(2,1)}, bf16[128,128]{1,0:T(8,128)(2,1)}) async-done(((bf16[128,128]{1,0:T(8,128)(2,1)}, bf16[128,128]{1,0:T(8,128)(2,1)}, bf16[128,128]{1,0:T(8,128)(2,1)}, bf16[128,128]{1,0:T(8,128)(2,1)}), (bf16[128,128]{1,0:T(8,128)(2,1)}, bf16[128,128]{1,0:T(8,128)(2,1)}, ...) | async-done | bytes 131088 | tf_op jit(solution)/shard_map/psum | solution.py:11
  550.8 1.0 fusion.83
  551.8 13.2 %convolution_subtract_fusion.3 = f32[64,16384]{1,0:T(8,128)S(1)} fusion(f32[64,16384]{1,0:T(8,128)} %bitcast.50, f32[64,128]{1,0:T(8,128)S(1)} %fusion.83, bf16[16384,128]{1,0:T(8,128)(2,1)} %get-tuple-element.9, s32[]{:T(128)} %bitcast.3, s32[16384]{0:T(1024)S(1)} %iota_add_fusion), kind=kOutput, calls=%fused_computation.3 | convolution fusion | flops 1626341376 | bytes 12681220 | tf_op jit(solution)/shard_map/dot_general | solution.py:44
  565.0 2.0 copy-done.9
  567.0 7.5 fusion.13
  574.5 53.1 %psum.88 = f32[64,128]{1,0:T(8,128)S(1)} all-reduce(f32[64,128]{1,0:T(8,128)S(1)} %fusion.13), channel_id=1, replica_groups=mesh['row'=16,'col'=8] {'row'}, use_global_device_ids=true, to_apply=%region_4.5 | all-reduce | flops 8192 | bytes 65536 | tf_op jit(solution)/shard_map/psum | solution.py:37
  627.7 0.2 fusion.84
  627.9 13.2 %convolution_subtract_fusion.2 = f32[64,16384]{1,0:T(8,128)S(1)} fusion(f32[64,16384]{1,0:T(8,128)} %copy-done.9, f32[64,128]{1,0:T(8,128)S(1)} %fusion.84, bf16[16384,128]{1,0:T(8,128)(2,1)} %get-tuple-element.10, s32[]{:T(128)} %bitcast.8, s32[16384]{0:T(1024)S(1)} %iota_add_fusion), kind=kOutput, calls=%fused_computation.2 | convolution fusion | flops 1626341376 | bytes 12681220 | tf_op jit(solution)/shard_map/dot_general | solution.py:44
  641.1 2.0 copy-done.10
  643.1 7.6 fusion.14
  650.7 53.2 %psum.91 = f32[64,128]{1,0:T(8,128)S(1)} all-reduce(f32[64,128]{1,0:T(8,128)S(1)} %fusion.14), channel_id=1, replica_groups=mesh['row'=16,'col'=8] {'row'}, use_global_device_ids=true, to_apply=%region_7.8 | all-reduce | flops 8192 | bytes 65536 | tf_op jit(solution)/shard_map/psum | solution.py:37
  703.9 0.2 fusion.85
  704.1 13.3 %convolution_subtract_fusion.1 = f32[64,16384]{1,0:T(8,128)S(1)} fusion(f32[64,16384]{1,0:T(8,128)} %copy-done.10, f32[64,128]{1,0:T(8,128)S(1)} %fusion.85, bf16[16384,128]{1,0:T(8,128)(2,1)} %get-tuple-element.11, s32[]{:T(128)} %bitcast.12, s32[16384]{0:T(1024)S(1)} %iota_add_fusion), kind=kOutput, calls=%fused_computation.1 | convolution fusion | flops 1626341376 | bytes 12681220 | tf_op jit(solution)/shard_map/dot_general | solution.py:44
  717.4 2.0 copy-done.8
  719.4 7.6 fusion.15
  727.0 52.9 %psum.94 = f32[64,128]{1,0:T(8,128)S(1)} all-reduce(f32[64,128]{1,0:T(8,128)S(1)} %fusion.15), channel_id=1, replica_groups=mesh['row'=16,'col'=8] {'row'}, use_global_device_ids=true, to_apply=%region_10.11 | all-reduce | flops 8192 | bytes 65536 | tf_op jit(solution)/shard_map/psum | solution.py:37
  779.9 0.2 fusion.86
  780.1 14.0 %convolution_subtract_fusion = f32[64,16384]{1,0:T(8,128)} fusion(f32[64,16384]{1,0:T(8,128)} %copy-done.8, f32[64,128]{1,0:T(8,128)S(1)} %fusion.86, bf16[16384,128]{1,0:T(8,128)(2,1)} %get-tuple-element.12, s32[]{:T(128)} %bitcast.16, s32[16384]{0:T(1024)S(1)} %iota_add_fusion), kind=kOutput, calls=%fused_computation | convolution fusion | flops 1626341376 | bytes 12681220 | tf_op jit(solution)/shard_map/dot_general | solution.py:44
  (22 shorter events, 0.1 us)
Async XLA Ops:
  6.5 454.8 %all-reduce.7.cloned.1.call-start = ((), (), s32[]{:S(2)}) async-start(), calls=%async_computation.3 | async-start | bytes 33554432 | tf_op jit(solution)/shard_map/psum | solution.py:11
  244.8 4.8 copy-start.3
  244.8 5.5 copy-start.4
  244.8 105.8 %all-to-all-start.1 = ((f32[8,64,2048]{2,1,0:T(8,128)}), f32[8,64,2048]{2,1,0:T(8,128)}, u32[]{:S(2)}, u32[]{:S(2)}) async-start(f32[8,64,2048]{2,1,0:T(8,128)} %all_to_all.29), calls=%async_computation.1 | async-start | bytes 8388608 | tf_op jit(solution)/shard_map/all_to_all | solution.py:25
  249.5 301.3 %all-reduce.5.cloned.1.call-start = ((), (), s32[]{:S(2)}) async-start(), calls=%async_computation.2 | async-start | bytes 262144 | tf_op jit(solution)/shard_map/psum | solution.py:11
  551.8 15.2 %copy-start.7 = (bf16[16384,128]{1,0:T(8,128)(2,1)S(1)}, bf16[16384,128]{1,0:T(8,128)(2,1)}, u32[]{:S(2)}) copy-start(bf16[16384,128]{1,0:T(8,128)(2,1)} %get-tuple-element.10) | copy-start | bytes 12582916
  565.0 2.0 copy-start.9
  567.0 60.7 %copy-start.2 = (bf16[128,128]{1,0:T(8,128)(2,1)S(1)}, bf16[128,128]{1,0:T(8,128)(2,1)}, u32[]{:S(2)}) copy-start(bf16[128,128]{1,0:T(8,128)(2,1)} %get-tuple-element.6) | copy-start | bytes 98308
  627.9 15.2 %copy-start.6 = (bf16[16384,128]{1,0:T(8,128)(2,1)S(1)}, bf16[16384,128]{1,0:T(8,128)(2,1)}, u32[]{:S(2)}) copy-start(bf16[16384,128]{1,0:T(8,128)(2,1)} %get-tuple-element.11) | copy-start | bytes 12582916
  641.1 2.0 copy-start.10
  643.1 60.8 %copy-start.1 = (bf16[128,128]{1,0:T(8,128)(2,1)S(1)}, bf16[128,128]{1,0:T(8,128)(2,1)}, u32[]{:S(2)}) copy-start(bf16[128,128]{1,0:T(8,128)(2,1)} %get-tuple-element.7) | copy-start | bytes 98308
  704.1 15.3 %copy-start.5 = (bf16[16384,128]{1,0:T(8,128)(2,1)S(1)}, bf16[16384,128]{1,0:T(8,128)(2,1)}, u32[]{:S(2)}) copy-start(bf16[16384,128]{1,0:T(8,128)(2,1)} %get-tuple-element.12) | copy-start | bytes 12582916
  717.4 2.0 copy-start.8
  719.4 60.6 %copy-start = (bf16[128,128]{1,0:T(8,128)(2,1)S(1)}, bf16[128,128]{1,0:T(8,128)(2,1)}, u32[]{:S(2)}) copy-start(bf16[128,128]{1,0:T(8,128)(2,1)} %get-tuple-element.8) | copy-start | bytes 98308
Sparse Core Ops, SparseCore 0:
  18.1 443.1 all-reduce.6
  464.0 86.7 all-reduce.4
where the time goes:
time: 812 us; the launch traced here: 801 us
  blocking collectives  436 us (54%)
  waiting for transfers between devices  224 us (28%)
  matrix products  94.4 us (12%)
  local copies, waits for them, and re-layouts  18.1 us (2%)
  between operations  16.5 us (2%)
    all_to_all x1, blocking collectives, local(): lax.all_to_all(eigvecs, ('row', 'col'), split_axis=1, concat_axis=0, tile...  222 us
    psum x4, blocking collectives, local(): projection = lax.psum(partial_sum, 'row')  214 us
    psum x2, waiting for transfers between devices, from_root(): return lax.psum(jnp.where(mine, value, jnp.zeros_like(value)), axis)  124 us
    all_to_all x1, waiting for transfers between devices, local(): lax.all_to_all(spread, 'col', split_axis=0, concat_axis=1, tiled=True)  99.6 us
    dot_general x4, matrix products, local(): jnp.dot(coeffs, reflector.T, precision=highest, preferred_element_type=jn...  53.6 us
    dot_general x4, matrix products, local(): jnp.dot(field, reflector, precision=highest, preferred_element_type=jnp.f...  39.2 us
  transfers between devices with their start and end apart: 3, of which 3 were waited for; matrix products, arithmetic and copies ran while one was open for 3% of the time, Pallas kernels for 0%

commit v1 on v0

--- a/solution.py
+++ b/solution.py
@@ -34,7 +34,7 @@
         partial_sum = jnp.dot(
             field, reflector, precision=highest, preferred_element_type=jnp.float32
         )
-        projection = lax.psum(partial_sum, "row")
+        projection = jnp.sum(lax.all_gather(partial_sum, "row"), axis=0)
         coeffs = jnp.dot(
             projection,
             triangle.astype(jnp.float32).T,

time: 812 us -> 703 us (0.87)
  blocking collectives: 436 us -> 299 us
  waiting for transfers between devices: 224 us -> 264 us
    psum x4 -> x0, blocking collectives: 214 us -> none  [local(): projection = lax.psum(partial_sum, 'row')]
    all_gather x0 -> x4, blocking collectives: none -> 77.4 us  [local(): projection = jnp.sum(lax.all_gather(partial_sum, 'row'), axis=0)]
    psum x2, waiting for transfers between devices: 124 us -> 165 us  [from_root(): return lax.psum(jnp.where(mine, value, jnp.zeros_like(value)), axis)]
  transfers between devices with their start and end apart: 3 -> 3, of which waited for: 3 -> 3; matrix products, arithmetic and copies ran while one was open for 3% -> 2% of each run, Pallas kernels for 0% -> 0%
where the time goes in v1:
time: 703 us; the launch traced here: 694 us
  blocking collectives  299 us (43%)
  waiting for transfers between devices  264 us (38%)
  matrix products  88.9 us (13%)
  between operations  16.4 us (2%)
  local copies, waits for them, and re-layouts  12.1 us (2%)
  other arithmetic  8.23 us (1%)
    all_to_all x1, blocking collectives, local(): lax.all_to_all(eigvecs, ('row', 'col'), split_axis=1, concat_axis=0, tile...  222 us
    psum x2, waiting for transfers between devices, from_root(): return lax.psum(jnp.where(mine, value, jnp.zeros_like(value)), axis)  165 us
    all_to_all x1, waiting for transfers between devices, local(): lax.all_to_all(spread, 'col', split_axis=0, concat_axis=1, tiled=True)  99.6 us
    all_gather x4, blocking collectives, local(): projection = jnp.sum(lax.all_gather(partial_sum, 'row'), axis=0)  77.4 us
    dot_general x4, matrix products, local(): jnp.dot(coeffs, reflector.T, precision=highest, preferred_element_type=jn...  53.6 us
    dot_general x4, matrix products, local(): jnp.dot(field, reflector, precision=highest, preferred_element_type=jnp.f...  33.7 us
  transfers between devices with their start and end apart: 3, of which 3 were waited for; matrix products, arithmetic and copies ran while one was open for 2% of the time, Pallas kernels for 0%

profile of v1, /device:TPU:0, one launch (start us, length us, event | category | flops | bytes accessed | tf_op | source)
XLA Modules:
  0.0 693.7 jit_solution(15025204466043644712)
XLA Ops:
  6.5 1.5 fusion.82
  10.5 7.4 %select_bitcast_fusion = (bf16[16384,128]{1,0:T(8,128)(2,1)}, bf16[16384,128]{1,0:T(8,128)(2,1)}, bf16[16384,128]{1,0:T(8,128)(2,1)}, bf16[16384,128]{1,0:T(8,128)(2,1)}) fusion(bf16[1,16384,128]{2,1,0:T(8,128)(2,1)} %param.6, pred[]{:T(512)S(6)} %eq.34, pred[]{:T(512)S(6)} %eq.30, pred[]{:T(512)S(6)} %eq.28, pred[]{:T(512)S(6)} %eq.32), kind=kLoop, calls=%fused_computation.25 | loop fusion | flops 8388608 | bytes 20971524 | tf_op jit(solution)/shard_map/jit(_where)/select_n | solution.py:11
  18.0 0.0 all-reduce.7.cloned.1.call-update
  18.0 221.5 %all_to_all.35 = f32[4,128,2048]{2,0,1:T(4,128)} all-to-all(f32[4,128,2048]{2,0,1:T(4,128)} %bitcast.52), channel_id=1, replica_groups=mesh['row'=16,'col'=8] {'row','col'}, dimensions={1} | all-to-all | bytes 8388608 | tf_op jit(solution)/shard_map/all_to_all | solution.py:24
  239.5 5.3 all_to_all.29
  244.8 4.7 all-to-all-start.1
  249.5 0.0 all-reduce.5.cloned.1.call-start
  249.6 0.7 select_bitcast_fusion.4
  250.2 0.0 all-reduce.5.cloned.1.call-update
  250.3 0.7 fusion.81
  251.0 99.6 %all-to-all-done.1 = f32[8,64,2048]{2,1,0:T(8,128)} async-done(((f32[8,64,2048]{2,1,0:T(8,128)}), f32[8,64,2048]{2,1,0:T(8,128)}, u32[]{:S(2)}, u32[]{:S(2)}) %all-to-all-start.1) | async-done | bytes 4194336 | tf_op jit(solution)/shard_map/all_to_all | solution.py:25
  350.6 4.7 copy.8
  355.3 106.0 %all-reduce.7.cloned.1.call-done = (bf16[16384,128]{1,0:T(8,128)(2,1)}, bf16[16384,128]{1,0:T(8,128)(2,1)}, bf16[16384,128]{1,0:T(8,128)(2,1)}, bf16[16384,128]{1,0:T(8,128)(2,1)}) async-done(((bf16[16384,128]{1,0:T(8,128)(2,1)}, bf16[16384,128]{1,0:T(8,128)(2,1)}, bf16[16384,128]{1,0:T(8,128)(2,1)}, bf16[16384,128]{1,0:T(8,128)(2,1)}), (bf16[16384,128]{1,0:T(8,128)(2,1)}, bf16[16384,128]{1,0:T(8,128)(2,1)}, ...) | async-done | bytes 16777232 | tf_op jit(solution)/shard_map/psum | solution.py:11
  461.3 10.8 %fusion.56 = f32[64,128]{1,0:T(8,128)S(1)} fusion(f32[64,16384]{1,0:T(8,128)} %bitcast.53, bf16[16384,128]{1,0:T(8,128)(2,1)} %get-tuple-element.9, s32[]{:T(128)} %bitcast.3, s32[16384]{0:T(1024)S(1)} %iota_add_fusion), kind=kOutput, calls=%fused_computation.69 | convolution fusion | flops 1625292800 | bytes 8486916 | tf_op jit(solution)/shard_map/dot_general | solution.py:34
  472.2 20.0 %all-gather = f32[1024,128]{1,0:T(8,128)S(1)} all-gather(f32[64,128]{1,0:T(8,128)S(1)} %fusion.56), channel_id=2, replica_groups=mesh['row'=16,'col'=8] {'row'}, dimensions={0}, use_global_device_ids=true | all-gather | bytes 557056 | tf_op jit(solution)/shard_map/all_gather | solution.py:37
  492.1 58.7 %all-reduce.5.cloned.1.call-done = (bf16[128,128]{1,0:T(8,128)(2,1)}, bf16[128,128]{1,0:T(8,128)(2,1)}, bf16[128,128]{1,0:T(8,128)(2,1)}, bf16[128,128]{1,0:T(8,128)(2,1)}) async-done(((bf16[128,128]{1,0:T(8,128)(2,1)}, bf16[128,128]{1,0:T(8,128)(2,1)}, bf16[128,128]{1,0:T(8,128)(2,1)}, bf16[128,128]{1,0:T(8,128)(2,1)}), (bf16[128,128]{1,0:T(8,128)(2,1)}, bf16[128,128]{1,0:T(8,128)(2,1)}, ...) | async-done | bytes 131088 | tf_op jit(solution)/shard_map/psum | solution.py:11
  550.8 0.9 fusion.83
  551.8 13.2 %convolution_subtract_fusion.3 = f32[64,16384]{1,0:T(8,128)S(1)} fusion(f32[64,16384]{1,0:T(8,128)} %bitcast.54, f32[64,128]{1,0:T(8,128)S(1)} %fusion.83, bf16[16384,128]{1,0:T(8,128)(2,1)} %get-tuple-element.9, s32[]{:T(128)} %bitcast.3, s32[16384]{0:T(1024)S(1)} %iota_add_fusion), kind=kOutput, calls=%fused_computation.3 | convolution fusion | flops 1626341376 | bytes 12681220 | tf_op jit(solution)/shard_map/dot_general | solution.py:44
  565.0 7.6 %fusion.13 = f32[64,128]{1,0:T(8,128)S(1)} fusion(f32[64,16384]{1,0:T(8,128)S(1)} %convolution_subtract_fusion.3, bf16[16384,128]{1,0:T(8,128)(2,1)S(1)} %copy-done.7, s32[]{:T(128)} %bitcast.9, s32[16384]{0:T(1024)S(1)} %iota_add_fusion), kind=kOutput, calls=%fused_computation.22 | convolution fusion | flops 1625292800 | bytes 8486916 | tf_op jit(solution)/shard_map/dot_general | solution.py:34
  572.6 20.5 %all-gather.1 = f32[1024,128]{1,0:T(8,128)S(1)} all-gather(f32[64,128]{1,0:T(8,128)S(1)} %fusion.13), channel_id=3, replica_groups=mesh['row'=16,'col'=8] {'row'}, dimensions={0}, use_global_device_ids=true | all-gather | bytes 557056 | tf_op jit(solution)/shard_map/all_gather | solution.py:37
  593.1 0.2 fusion.84
  593.3 13.2 %convolution_subtract_fusion.2 = f32[64,16384]{1,0:T(8,128)S(1)} fusion(f32[64,16384]{1,0:T(8,128)} %copy-done.9, f32[64,128]{1,0:T(8,128)S(1)} %fusion.84, bf16[16384,128]{1,0:T(8,128)(2,1)} %get-tuple-element.10, s32[]{:T(128)} %bitcast.9, s32[16384]{0:T(1024)S(1)} %iota_add_fusion), kind=kOutput, calls=%fused_computation.2 | convolution fusion | flops 1626341376 | bytes 12681220 | tf_op jit(solution)/shard_map/dot_general | solution.py:44
  606.5 0.0 copy-start.10
  606.5 7.6 %fusion.14 = f32[64,128]{1,0:T(8,128)S(1)} fusion(f32[64,16384]{1,0:T(8,128)S(1)} %convolution_subtract_fusion.2, bf16[16384,128]{1,0:T(8,128)(2,1)S(1)} %copy-done.6, s32[]{:T(128)} %bitcast.14, s32[16384]{0:T(1024)S(1)} %iota_add_fusion), kind=kOutput, calls=%fused_computation.23 | convolution fusion | flops 1625292800 | bytes 8486916 | tf_op jit(solution)/shard_map/dot_general | solution.py:34
  614.2 17.9 %all-gather.2 = f32[1024,128]{1,0:T(8,128)S(1)} all-gather(f32[64,128]{1,0:T(8,128)S(1)} %fusion.14), channel_id=4, replica_groups=mesh['row'=16,'col'=8] {'row'}, dimensions={0}, use_global_device_ids=true | all-gather | bytes 557056 | tf_op jit(solution)/shard_map/all_gather | solution.py:37
  632.2 0.2 fusion.85
  632.4 13.3 %convolution_subtract_fusion.1 = f32[64,16384]{1,0:T(8,128)S(1)} fusion(f32[64,16384]{1,0:T(8,128)} %copy-done.10, f32[64,128]{1,0:T(8,128)S(1)} %fusion.85, bf16[16384,128]{1,0:T(8,128)(2,1)} %get-tuple-element.11, s32[]{:T(128)} %bitcast.14, s32[16384]{0:T(1024)S(1)} %iota_add_fusion), kind=kOutput, calls=%fused_computation.1 | convolution fusion | flops 1626341376 | bytes 12681220 | tf_op jit(solution)/shard_map/dot_general | solution.py:44
  645.7 0.0 copy-start.8
  645.7 7.7 %fusion.15 = f32[64,128]{1,0:T(8,128)S(1)} fusion(f32[64,16384]{1,0:T(8,128)S(1)} %convolution_subtract_fusion.1, bf16[16384,128]{1,0:T(8,128)(2,1)S(1)} %copy-done.5, s32[]{:T(128)} %bitcast.19, s32[16384]{0:T(1024)S(1)} %iota_add_fusion), kind=kOutput, calls=%fused_computation.24 | convolution fusion | flops 1625292800 | bytes 8486916 | tf_op jit(solution)/shard_map/dot_general | solution.py:34
  653.4 19.0 %all-gather.3 = f32[1024,128]{1,0:T(8,128)S(1)} all-gather(f32[64,128]{1,0:T(8,128)S(1)} %fusion.15), channel_id=5, replica_groups=mesh['row'=16,'col'=8] {'row'}, dimensions={0}, use_global_device_ids=true | all-gather | bytes 557056 | tf_op jit(solution)/shard_map/all_gather | solution.py:37
  672.5 0.2 fusion.86
  672.7 14.0 %convolution_subtract_fusion = f32[64,16384]{1,0:T(8,128)} fusion(f32[64,16384]{1,0:T(8,128)} %copy-done.8, f32[64,128]{1,0:T(8,128)S(1)} %fusion.86, bf16[16384,128]{1,0:T(8,128)(2,1)} %get-tuple-element.12, s32[]{:T(128)} %bitcast.19, s32[16384]{0:T(1024)S(1)} %iota_add_fusion), kind=kOutput, calls=%fused_computation | convolution fusion | flops 1626341376 | bytes 12681220 | tf_op jit(solution)/shard_map/dot_general | solution.py:44
  (26 shorter events, 0.2 us)
Async XLA Ops:
  6.5 454.8 %all-reduce.7.cloned.1.call-start = ((), (), s32[]{:S(2)}) async-start(), calls=%async_computation.3 | async-start | bytes 33554432 | tf_op jit(solution)/shard_map/psum | solution.py:11
  244.8 4.8 copy-start.3
  244.8 5.5 copy-start.4
  244.8 105.8 %all-to-all-start.1 = ((f32[8,64,2048]{2,1,0:T(8,128)}), f32[8,64,2048]{2,1,0:T(8,128)}, u32[]{:S(2)}, u32[]{:S(2)}) async-start(f32[8,64,2048]{2,1,0:T(8,128)} %all_to_all.29), calls=%async_computation.1 | async-start | bytes 8388608 | tf_op jit(solution)/shard_map/all_to_all | solution.py:25
  249.5 301.3 %all-reduce.5.cloned.1.call-start = ((), (), s32[]{:S(2)}) async-start(), calls=%async_computation.2 | async-start | bytes 262144 | tf_op jit(solution)/shard_map/psum | solution.py:11
  551.8 13.2 %copy-start.7 = (bf16[16384,128]{1,0:T(8,128)(2,1)S(1)}, bf16[16384,128]{1,0:T(8,128)(2,1)}, u32[]{:S(2)}) copy-start(bf16[16384,128]{1,0:T(8,128)(2,1)} %get-tuple-element.10) | copy-start | bytes 12582916
  565.0 7.6 %copy-start.9 = (f32[64,16384]{1,0:T(8,128)}, f32[64,16384]{1,0:T(8,128)S(1)}, u32[]{:S(2)}) copy-start(f32[64,16384]{1,0:T(8,128)S(1)} %convolution_subtract_fusion.3) | copy-start | bytes 12582916
  565.0 28.1 %copy-start.2 = (bf16[128,128]{1,0:T(8,128)(2,1)S(1)}, bf16[128,128]{1,0:T(8,128)(2,1)}, u32[]{:S(2)}) copy-start(bf16[128,128]{1,0:T(8,128)(2,1)} %get-tuple-element.6) | copy-start | bytes 98308
  593.3 13.2 %copy-start.6 = (bf16[16384,128]{1,0:T(8,128)(2,1)S(1)}, bf16[16384,128]{1,0:T(8,128)(2,1)}, u32[]{:S(2)}) copy-start(bf16[16384,128]{1,0:T(8,128)(2,1)} %get-tuple-element.11) | copy-start | bytes 12582916
  606.5 7.7 %copy-start.10 = (f32[64,16384]{1,0:T(8,128)}, f32[64,16384]{1,0:T(8,128)S(1)}, u32[]{:S(2)}) copy-start(f32[64,16384]{1,0:T(8,128)S(1)} %convolution_subtract_fusion.2) | copy-start | bytes 12582916
  606.5 25.6 %copy-start.1 = (bf16[128,128]{1,0:T(8,128)(2,1)S(1)}, bf16[128,128]{1,0:T(8,128)(2,1)}, u32[]{:S(2)}) copy-start(bf16[128,128]{1,0:T(8,128)(2,1)} %get-tuple-element.7) | copy-start | bytes 98308
  632.4 13.3 %copy-start.5 = (bf16[16384,128]{1,0:T(8,128)(2,1)S(1)}, bf16[16384,128]{1,0:T(8,128)(2,1)}, u32[]{:S(2)}) copy-start(bf16[16384,128]{1,0:T(8,128)(2,1)} %get-tuple-element.12) | copy-start | bytes 12582916
  645.7 7.7 %copy-start.8 = (f32[64,16384]{1,0:T(8,128)}, f32[64,16384]{1,0:T(8,128)S(1)}, u32[]{:S(2)}) copy-start(f32[64,16384]{1,0:T(8,128)S(1)} %convolution_subtract_fusion.1) | copy-start | bytes 12582916
  645.7 26.8 %copy-start = (bf16[128,128]{1,0:T(8,128)(2,1)S(1)}, bf16[128,128]{1,0:T(8,128)(2,1)}, u32[]{:S(2)}) copy-start(bf16[128,128]{1,0:T(8,128)(2,1)} %get-tuple-element.8) | copy-start | bytes 98308
Sparse Core Ops, SparseCore 0:
  18.1 443.1 all-reduce.6
  464.0 86.7 all-reduce.4
